TPU v7x, 512 devices: a whole 4x8x8 slice. The times are simulated.
512 devices in a mesh: dp: 64 (over z, x, core), expert: 8 (over y).
Axes of the slice: x: 4, y: 8, z: 8, core: 2. Of those that a mesh axis runs over, the one named last changes fastest.
Arguments:
- tokens: bfloat16 [512, 4096], P('expert', 'dp'), may hold values from -6 to 6
- cotangent: bfloat16 [512, 4096], P('expert', 'dp'), may hold values from -6 to 6
- gate_logit: float32 [512], P('expert'), may hold values from -8 to 8
- routes: int32 [512, 2], P('expert'), may hold values from 0 to 7, all different within a row; in each aligned block of 64 rows (0 to 63, 64 to 127, ...) at most 32 rows name the same one
- w_up: bfloat16 [8, 14336, 4096], P('expert', 'dp'), may hold values from -0.09375 to 0.09375
- w_down: bfloat16 [8, 14336, 4096], P('expert', 'dp'), may hold values from -0.046875 to 0.046875
- basis: bfloat16 [4096, 256], P('dp'), may hold values from -0.09375 to 0.09375
- sketch: float32 [8, 256, 256], P('expert'), may hold values from -1 to 10, as said below
Outputs:
- token_grad: bfloat16 [512, 4096], P('expert', 'dp')
- sketch_next: float32 [8, 256, 256], P('expert')
- precond: float32 [8, 14336, 256], P('expert', 'dp')
Inputs may be any that keep to these rules, and one draw needn't show every extreme that they name: `routes`: each row names 2 different experts. Among the 64 tokens of one index of expert at most 32 name the same expert, and in some index that many do. `sketch`: each matrix is symmetric, and in every row its diagonal entry exceeds the sum of the magnitudes off the diagonal.
All inputs are finite; a program needn't handle non-finite values.
Results may differ from a plain program's by a relative error of at most 0.0064.
Values may be sent and summed in bfloat16 or wider, within the bound.
A program may use at most 128 MiB of HBM per device.

v0:
```python
import jax
import jax.numpy as jnp
from jax import lax
from jax.sharding import PartitionSpec as P

decay_rate = 0.9
damping = 1.0
highest = lax.Precision.HIGHEST


def per_device(tokens, cotangent, gate_logit, routes, w_up, w_down, basis, sketch):
    experts = lax.axis_size("expert")
    tok_rows = tokens.shape[0]
    width_local = tokens.shape[1]
    capacity = min(tok_rows, tok_rows * 4 // experts)
    slot_count = experts * capacity
    gate_first = jax.nn.sigmoid(gate_logit)
    gates = jnp.stack([gate_first, 1.0 - gate_first], axis=1)
    expert_ids = jnp.arange(experts, dtype=jnp.int32)
    chosen = routes[:, :, None] == expert_ids[None, None, :]
    hit_count = jnp.sum(chosen.astype(jnp.int32), axis=1)
    gate_by_expert = jnp.sum(chosen.astype(jnp.float32) * gates[:, :, None], axis=1)
    before = jnp.cumsum(hit_count, axis=0) - hit_count
    slot_of = expert_ids[None, :] * capacity + before
    slot_ids = jnp.arange(slot_count, dtype=jnp.int32)
    slot_match = (
        (slot_of[None, :, :] == slot_ids[:, None, None]) & (hit_count[None, :, :] > 0)
    ).astype(jnp.float32)
    table = jnp.sum(slot_match, axis=2)
    gate_slot = jnp.sum(slot_match * gate_by_expert[None, :, :], axis=(1, 2))
    table_b = table.astype(jnp.bfloat16)
    x_send = jnp.dot(table_b, tokens, preferred_element_type=jnp.float32).astype(jnp.bfloat16)
    cot_rows = jnp.dot(table_b, cotangent, preferred_element_type=jnp.float32)
    dy_send = (gate_slot[:, None] * cot_rows).astype(jnp.bfloat16)
    x_send = x_send.reshape(experts, capacity, width_local)
    dy_send = dy_send.reshape(experts, capacity, width_local)
    x_recv, dy_recv = (
        lax.all_to_all(x_send, "expert", split_axis=0, concat_axis=0, tiled=True),
        lax.all_to_all(dy_send, "expert", split_axis=0, concat_axis=0, tiled=True),
    )
    x_full, dy_full = (
        lax.all_gather(x_recv, "dp", axis=2, tiled=True),
        lax.all_gather(dy_recv, "dp", axis=2, tiled=True),
    )
    row_block = x_full.reshape(slot_count, -1)
    dy_block = dy_full.reshape(slot_count, -1)
    up_local = w_up[0]
    down_local = w_down[0]
    hidden = lax.dot_general(
        row_block, up_local, (((1,), (1,)), ((), ())), preferred_element_type=jnp.float32
    )
    back_grad = lax.dot_general(
        dy_block, down_local, (((1,), (1,)), ((), ())), preferred_element_type=jnp.float32
    )
    sigma_val = jax.nn.sigmoid(hidden)
    hidden_grad = (back_grad * sigma_val * (1.0 + hidden * (1.0 - sigma_val))).astype(jnp.bfloat16)
    partial_value = jnp.dot(hidden_grad, up_local, preferred_element_type=jnp.float32)
    summed = lax.psum_scatter(partial_value, "dp", scatter_dimension=1, tiled=True).astype(
        jnp.bfloat16
    )
    returned = lax.all_to_all(
        summed.reshape(experts, capacity, width_local),
        "expert",
        split_axis=0,
        concat_axis=0,
        tiled=True,
    )
    token_grad = lax.dot_general(
        table_b,
        returned.reshape(slot_count, width_local),
        (((0,), (0,)), ((), ())),
        preferred_element_type=jnp.float32,
    ).astype(jnp.bfloat16)
    basis_full = lax.all_gather(basis, "dp", axis=0, tiled=True)
    projected = jnp.dot(row_block, basis_full, preferred_element_type=jnp.float32).astype(
        jnp.bfloat16
    )
    coefficients = lax.dot_general(
        projected, hidden_grad, (((0,), (0,)), ((), ())), preferred_element_type=jnp.float32
    )
    gram_part = jnp.dot(coefficients, coefficients.T, precision=highest)
    total_hidden = w_up.shape[1] * lax.axis_size("dp")
    gram_total = lax.psum(gram_part, "dp") / total_hidden
    merged = decay_rate * sketch[0] + gram_total
    factor = jnp.linalg.cholesky(merged + damping * jnp.eye(merged.shape[0], dtype=jnp.float32))
    solved = damping * jax.scipy.linalg.cho_solve((factor, True), coefficients)
    return (token_grad, merged[None], solved.T[None])


def solution(mesh):
    in_specs = (
        P("expert", "dp"),
        P("expert", "dp"),
        P("expert"),
        P("expert", None),
        P("expert", "dp", None),
        P("expert", "dp", None),
        P("dp", None),
        P("expert", None, None),
    )
    out_specs = (P("expert", "dp"), P("expert", None, None), P("expert", "dp", None))
    return jax.shard_map(
        per_device, mesh=mesh, in_specs=in_specs, out_specs=out_specs, check_vma=False
    )
```

profile of v0, /device:TPU:2, one launch (start us, length us, event | category | flops | bytes accessed | tf_op | source)
XLA Modules:
  0.0 657.5 jit_solution(2081533431602891325)
XLA Ops:
  7.2 0.8 convert_reduce_fusion.1
  8.1 0.7 subtract_bitcast_fusion
  8.8 0.7 select_reduce_fusion.3
  9.6 0.1 copy.41
  9.7 0.1 reduce_window_sum.11
  9.8 0.3 convert_reduce_fusion
  10.1 0.9 fusion.16
  11.0 0.1 copy.43
  11.2 0.1 reshape.113
  11.3 14.9 %all_to_all.15 = bf16[8,2,1024]{2,1,0:T(2,128)(2,1)S(1)} all-to-all(bf16[8,2,1024]{2,1,0:T(2,128)(2,1)S(1)} %reshape.113), channel_id=1, replica_groups=mesh['dp'=64,'expert'=8] {'expert'}, dimensions={0} | all-to-all | bytes 65536 | tf_op jit(solution)/shard_map/all_to_all | solution.py:39
  26.2 0.1 reshape.114
  26.3 0.8 copy.44
  27.2 0.9 convolution_convert_fusion.1
  28.1 0.1 copy.46
  28.2 0.1 reshape.115
  28.3 10.4 %all_to_all.16 = bf16[8,2,1024]{2,1,0:T(2,128)(2,1)S(1)} all-to-all(bf16[8,2,1024]{2,1,0:T(2,128)(2,1)S(1)} %reshape.115), channel_id=1, replica_groups=mesh['dp'=64,'expert'=8] {'expert'}, dimensions={0} | all-to-all | bytes 65536 | tf_op jit(solution)/shard_map/all_to_all | solution.py:38
  38.7 0.1 reshape.116
  38.9 0.8 copy.47
  39.7 0.7 all-gather.8.cloned.1.call-update
  40.5 74.2 %all-gather.4.cloned.1.call-done = bf16[8,32,4096]{1,0,2:T(8,128)(2,1)} async-done(((bf16[8,32,64]{1,0,2:T(8,128)(2,1)}), bf16[8,32,4096]{1,0,2:T(8,128)(2,1)}) %all-gather.4.cloned.1.call-update) | async-done | bytes 2097168 | tf_op jit(solution)/shard_map/all_gather | solution.py:43
  114.7 9.3 %copy.45 = bf16[8,32,4096]{2,1,0:T(8,128)(2,1)} copy(bf16[8,32,4096]{1,0,2:T(8,128)(2,1)} %all-gather.4.cloned.1.call-done) | data formatting | bytes 4194304 | tf_op jit(solution)/shard_map/all_gather | solution.py:43
  124.0 80.1 %all-gather.6.cloned.1.call-done = bf16[8,32,4096]{1,0,2:T(8,128)(2,1)} async-done(((bf16[8,32,64]{1,0,2:T(8,128)(2,1)}), bf16[8,32,4096]{1,0,2:T(8,128)(2,1)}) %all-gather.6.cloned.1.call-update) | async-done | bytes 2097168 | tf_op jit(solution)/shard_map/all_gather | solution.py:42
  204.1 9.4 %copy.48 = bf16[8,32,4096]{2,1,0:T(8,128)(2,1)} copy(bf16[8,32,4096]{1,0,2:T(8,128)(2,1)} %all-gather.6.cloned.1.call-done) | data formatting | bytes 4194304 | tf_op jit(solution)/shard_map/all_gather | solution.py:42
  213.5 2.5 fusion.2
  216.1 0.2 copy-done.3
  216.3 0.8 fusion.12
  217.1 70.8 %all-gather.8.cloned.1.call-done = bf16[4096,256]{1,0:T(8,128)(2,1)} async-done(((bf16[64,256]{1,0:T(8,128)(2,1)}), bf16[4096,256]{1,0:T(8,128)(2,1)}) %all-gather.8.cloned.1.call-update) | async-done | bytes 2097168 | tf_op jit(solution)/shard_map/all_gather | solution.py:74
  287.8 3.1 fusion.15
  291.0 1.3 fusion.34
  292.4 0.2 reduce-scatter.2.cloned.1.call-start
  292.6 2.9 fusion
  295.5 0.9 copy-done.2
  296.4 0.1 copy.50
  296.6 181.5 %all-reduce.3.cloned.1.call-done = f32[256,256]{0,1:T(8,128)} async-done(((f32[256,256]{0,1:T(8,128)}), f32[256,256]{0,1:T(8,128)}) %all-reduce.3.cloned.1.call-update) | async-done | bytes 262160 | tf_op jit(solution)/shard_map/psum | solution.py:83
  478.1 1.0 convert_add_fusion
  479.1 0.1 copy.52
  479.3 11.7 %cholesky.50 = f32[128,128]{1,0:T(8,128)S(1)} custom-call(f32[128,128]{1,0:T(8,128)S(1)} %cholesky.118), custom_call_target="Cholesky" | custom-call | tf_op jit(solution)/shard_map/jit(cholesky)/cholesky | solution.py:85
  491.0 9.8 %custom-call.18 = f32[1,128,128]{1,2,0:T(8,128)S(1)} custom-call(f32[1,128,128]{2,1,0:T(8,128)S(1)} %get-tuple-element.42), custom_call_target="InvertDiagBlocksLowerTriangular" | custom-call | tf_op jit(solution)/shard_map/jit(cholesky)/cholesky | solution.py:85
  500.9 0.2 constant_dynamic-update-slice_fusion.1
  501.1 0.3 convolution_subtract_fusion.2
  501.3 11.7 %cholesky.105 = f32[128,128]{1,0:T(8,128)S(1)} custom-call(f32[128,128]{1,0:T(8,128)S(1)} %convolution_subtract_fusion.2), custom_call_target="Cholesky" | custom-call | tf_op jit(solution)/shard_map/jit(cholesky)/cholesky | solution.py:85
  513.1 0.6 compare_reduce_fusion
  515.1 4.2 while.1
  515.3 0.6 fusion.57
  515.9 1.4 bitcast_dynamic-update-slice_fusion.2
  517.3 0.6 fusion.57
  517.9 1.4 bitcast_dynamic-update-slice_fusion.2
  519.3 19.7 %custom-call.19 = f32[2,128,128]{1,2,0:T(8,128)S(1)} custom-call(f32[2,128,128]{2,1,0:T(8,128)S(1)} %get-tuple-element.10), custom_call_target="InvertDiagBlocksLowerTriangular" | custom-call | tf_op jit(solution)/shard_map/jit(_cho_solve)/triangular_solve | solution.py:86
  539.0 0.2 fusion.19
  539.3 0.3 convolution_subtract_fusion.1
  539.5 0.3 fusion.27
  539.8 0.3 fusion.26
  540.1 0.2 convolution_subtract_fusion
  540.3 0.3 fusion.25
  540.6 93.1 %reduce-scatter.2.cloned.1.call-done = f32[256,64]{0,1:T(8,128)} async-done(((f32[256,4096]{0,1:T(8,128)}), f32[256,64]{0,1:T(8,128)}) %reduce-scatter.2.cloned.1.call-update) | async-done | bytes 65552 | tf_op jit(solution)/shard_map/reduce_scatter | solution.py:58
  633.7 0.8 convert_element_type.37
  634.5 0.1 copy.49
  634.7 0.7 reshape.117
  635.4 6.7 %all-to-all-start.2 = ((bf16[8,2,1024]{2,1,0:T(2,128)(2,1)}), bf16[8,2,1024]{2,1,0:T(2,128)(2,1)S(1)}, u32[]{:S(2)}, u32[]{:S(2)}) async-start(bf16[8,2,1024]{2,1,0:T(2,128)(2,1)} %reshape.117), calls=%async_computation.3 | async-start | bytes 65536 | tf_op jit(solution)/shard_map/all_to_all | solution.py:61
  642.1 0.7 maximum_bitcast_fusion
  642.8 0.8 copy.53
  643.7 6.5 all-to-all-done.2
  650.1 0.1 reshape.118
  650.3 0.7 convolution_convert_fusion.2
  (31 shorter events, 0.7 us)
Async XLA Ops:
  7.2 206.4 %copy-start = (bf16[1,224,4096]{2,1,0:T(8,128)(2,1)S(1)}, bf16[1,224,4096]{2,1,0:T(8,128)(2,1)}, u32[]{:S(2)}) copy-start(bf16[1,224,4096]{2,1,0:T(8,128)(2,1)} %param.12) | copy-start | bytes 5505028
  7.2 107.5 %all-gather.4.cloned.1.call-start = ((), (), s32[]{:S(2)}) async-start(), calls=%async_computation.4 | async-start | bytes 8519680 | tf_op jit(solution)/shard_map/all_gather | solution.py:43
  27.1 177.0 %all-gather.6.cloned.1.call-start = ((), (), s32[]{:S(2)}) async-start(), calls=%async_computation.5 | async-start | bytes 8519680 | tf_op jit(solution)/shard_map/all_gather | solution.py:42
  39.7 248.2 %all-gather.8.cloned.1.call-start = ((), (), s32[]{:S(2)}) async-start(), calls=%async_computation.7 | async-start | bytes 2129920 | tf_op jit(solution)/shard_map/all_gather | solution.py:74
  40.4 437.7 %all-reduce.3.cloned.1.call-start = ((), (), s32[]{:S(2)}) async-start(), calls=%async_computation.8 | async-start | bytes 524288 | tf_op jit(solution)/shard_map/psum | solution.py:83
  213.5 2.6 copy-start.1
  213.5 2.8 copy-start.3
  292.4 341.3 %reduce-scatter.2.cloned.1.call-start = ((), (), s32[]{:S(2)}) async-start(), calls=%async_computation.6 | async-start | bytes 4259840 | tf_op jit(solution)/shard_map/reduce_scatter | solution.py:58
  295.5 0.9 copy-start.2
  635.4 14.8 %all-to-all-start.2 = ((bf16[8,2,1024]{2,1,0:T(2,128)(2,1)}), bf16[8,2,1024]{2,1,0:T(2,128)(2,1)S(1)}, u32[]{:S(2)}, u32[]{:S(2)}) async-start(bf16[8,2,1024]{2,1,0:T(2,128)(2,1)} %reshape.117), calls=%async_computation.3 | async-start | bytes 65536 | tf_op jit(solution)/shard_map/all_to_all | solution.py:61
Sparse Core Ops, SparseCore 0:
  27.3 87.3 all-gather.3
  118.6 85.4 all-gather.5
  207.5 80.3 all-gather.7
  292.5 185.5 all-reduce.2
  482.6 151.0 reduce-scatter.1
where the time goes:
time: 658 us
  waiting for transfers between devices  507 us (77%)
  other arithmetic  58.9 us (9%)
  local copies, waits for them, and re-layouts  28.5 us (4%)
  blocking collectives  25.3 us (4%)
  matrix products  15.3 us (2%)
  between operations  15.3 us (2%)
  starting transfers between devices  7.12 us (1%)
    psum x1, waiting for transfers between devices, per_device(): gram_total = lax.psum(gram_part, 'dp') / total_hidden  181 us
    reduce_scatter x1, waiting for transfers between devices, per_device(): lax.psum_scatter(partial_value, 'dp', scatter_dimension=1, tiled=True)  93.1 us
    all_gather x1, waiting for transfers between devices, per_device(): lax.all_gather(x_recv, 'dp', axis=2, tiled=True)  80.1 us
    all_gather x1, waiting for transfers between devices, per_device(): lax.all_gather(dy_recv, 'dp', axis=2, tiled=True)  74.2 us
    all_gather x1, waiting for transfers between devices, per_device(): basis_full = lax.all_gather(basis, 'dp', axis=0, tiled=True)  70.8 us
    another operation x6, other arithmetic, per_device(): jnp.linalg.cholesky(merged + damping * jnp.eye(merged.shape[0], dtype=jnp...  34 us
    another operation x3, other arithmetic, per_device(): solved = damping * jax.scipy.linalg.cho_solve((factor, True), coefficients)  19.7 us
    all_to_all x1, blocking collectives, per_device(): lax.all_to_all(dy_send, 'expert', split_axis=0, concat_axis=0, tiled=True)  14.9 us
  transfers between devices with their start and end apart: 6, of which 6 were waited for; matrix products, arithmetic and copies ran while one was open for 14% of the time, Pallas kernels for 0%

commit v1 on v0

--- a/solution.py
+++ b/solution.py
@@ -6,6 +6,13 @@
 decay_rate = 0.9
 damping = 1.0
 highest = lax.Precision.HIGHEST
+
+
+def _reach_meshes(mesh_dim, matrix):
+    outcome_arr = jnp.stack([matrix for _ in range(lax.axis_size(mesh_dim))])
+    wide_out = lax.all_to_all(outcome_arr, mesh_dim, split_axis=0, concat_axis=0)
+    built = jnp.concatenate(wide_out, 2)
+    return built
 
 
 def per_device(tokens, cotangent, gate_logit, routes, w_up, w_down, basis, sketch):
@@ -39,7 +46,7 @@
         lax.all_to_all(dy_send, "expert", split_axis=0, concat_axis=0, tiled=True),
     )
     x_full, dy_full = (
-        lax.all_gather(x_recv, "dp", axis=2, tiled=True),
+        _reach_meshes("dp", x_recv),
         lax.all_gather(dy_recv, "dp", axis=2, tiled=True),
     )
     row_block = x_full.reshape(slot_count, -1)

time: 658 us -> 587 us (0.89)
  waiting for transfers between devices: 507 us -> 399 us
  local copies, waits for them, and re-layouts: 28.5 us -> 50.6 us
  starting transfers between devices: 7.12 us -> 21.4 us
    all_gather x1 -> x0, waiting for transfers between devices: 80.1 us -> none  [per_device(): lax.all_gather(x_recv, 'dp', axis=2, tiled=True)]
    all_gather x1, waiting for transfers between devices: 74.2 us -> 0.01 us  [per_device(): lax.all_gather(dy_recv, 'dp', axis=2, tiled=True)]
    all_to_all x0 -> x1, waiting for transfers between devices: none -> 62.2 us  [_reach_meshes(): lax.all_to_all(outcome_arr, mesh_dim, split_axis=0, concat_axis=0)]
    all_gather x1, waiting for transfers between devices: 70.8 us -> 54.7 us  [per_device(): basis_full = lax.all_gather(basis, 'dp', axis=0, tiled=True)]
    unnamed x16 -> x18, local copies, waits for them, and re-layouts: 3.36 us -> 19.2 us
    all_to_all x0 -> x1, starting transfers between devices: none -> 14.1 us  [_reach_meshes(): lax.all_to_all(outcome_arr, mesh_dim, split_axis=0, concat_axis=0)]
    another operation x6 -> x8, local copies, waits for them, and re-layouts: 3.96 us -> 13.6 us  [the longest x1 6.61 us: per_device(): row_block = x_full.reshape(slot_count, -1)]
    all_gather x1 -> x0, local copies, waits for them, and re-layouts: 9.39 us -> none  [per_device(): lax.all_gather(x_recv, 'dp', axis=2, tiled=True)]
  transfers between devices with their start and end apart: 6 -> 6, of which waited for: 6 -> 5; matrix products, arithmetic and copies ran while one was open for 14% -> 19% of each run, Pallas kernels for 0% -> 0%
where the time goes in v1:
time: 587 us; the launch traced here: 586 us
  waiting for transfers between devices  399 us (68%)
  other arithmetic  58.9 us (10%)
  local copies, waits for them, and re-layouts  50.6 us (9%)
  blocking collectives  25.3 us (4%)
  starting transfers between devices  21.4 us (4%)
  matrix products  15.3 us (3%)
  between operations  15.3 us (3%)
    psum x1, waiting for transfers between devices, per_device(): gram_total = lax.psum(gram_part, 'dp') / total_hidden  181 us
    reduce_scatter x1, waiting for transfers between devices, per_device(): lax.psum_scatter(partial_value, 'dp', scatter_dimension=1, tiled=True)  93.1 us
    all_to_all x1, waiting for transfers between devices, _reach_meshes(): lax.all_to_all(outcome_arr, mesh_dim, split_axis=0, concat_axis=0)  62.2 us
    all_gather x1, waiting for transfers between devices, per_device(): basis_full = lax.all_gather(basis, 'dp', axis=0, tiled=True)  54.7 us
    another operation x6, other arithmetic, per_device(): jnp.linalg.cholesky(merged + damping * jnp.eye(merged.shape[0], dtype=jnp...  34 us
    another operation x3, other arithmetic, per_device(): solved = damping * jax.scipy.linalg.cho_solve((factor, True), coefficients)  19.7 us
    unnamed x18, local copies, waits for them, and re-layouts  19.2 us
    all_to_all x1, blocking collectives, per_device(): lax.all_to_all(dy_send, 'expert', split_axis=0, concat_axis=0, tiled=True)  14.9 us
  transfers between devices with their start and end apart: 6, of which 5 were waited for; matrix products, arithmetic and copies ran while one was open for 19% of the time, Pallas kernels for 0%

profile of v1, /device:TPU:2, one launch (start us, length us, event | category | flops | bytes accessed | tf_op | source)
XLA Modules:
  0.0 585.7 jit_solution(10869261103043856527)
XLA Ops:
  7.2 0.8 convert_reduce_fusion.1
  8.1 0.7 subtract_bitcast_fusion
  8.8 0.7 select_reduce_fusion.3
  9.8 0.3 convert_reduce_fusion
  10.1 0.9 fusion.16
  11.0 0.1 copy.43
  11.2 0.1 reshape.115
  11.3 14.9 %all_to_all.20 = bf16[8,2,1024]{2,1,0:T(2,128)(2,1)S(1)} all-to-all(bf16[8,2,1024]{2,1,0:T(2,128)(2,1)S(1)} %reshape.115), channel_id=1, replica_groups=mesh['dp'=64,'expert'=8] {'expert'}, dimensions={0} | all-to-all | bytes 65536 | tf_op jit(solution)/shard_map/all_to_all | solution.py:46
  26.2 0.1 reshape.116
  26.3 0.8 copy.44
  27.1 0.9 convolution_convert_fusion.1
  28.1 0.1 copy.46
  28.2 0.1 reshape.117
  28.3 10.4 %all_to_all.21 = bf16[8,2,1024]{2,1,0:T(2,128)(2,1)S(1)} all-to-all(bf16[8,2,1024]{2,1,0:T(2,128)(2,1)S(1)} %reshape.117), channel_id=1, replica_groups=mesh['dp'=64,'expert'=8] {'expert'}, dimensions={0} | all-to-all | bytes 65536 | tf_op jit(solution)/shard_map/all_to_all | solution.py:45
  38.8 3.0 stack.11
  41.8 7.9 %reshape.119 = bf16[64,2,8192]{2,1,0:T(2,128)(2,1)} reshape(bf16[64,8,32,64]{3,2,1,0:T(8,128)(2,1)} %stack.11) | data formatting | bytes 4194304
  49.7 14.1 %all-to-all-start.2 = ((bf16[64,2,8192]{2,1,0:T(2,128)(2,1)}), bf16[64,2,8192]{2,1,0:T(2,128)(2,1)}, u32[]{:S(2)}, u32[]{:S(2)}) async-start(bf16[64,2,8192]{2,1,0:T(2,128)(2,1)} %reshape.119), calls=%async_computation.2 | async-start | bytes 4194304 | tf_op jit(solution)/shard_map/all_to_all | solution.py:13
  63.8 0.7 all-gather.5.cloned.1.call-update
  64.5 0.2 all-reduce.3.cloned.1.call-start
  64.7 62.2 %all-to-all-done.2 = bf16[64,2,8192]{2,1,0:T(2,128)(2,1)} async-done(((bf16[64,2,8192]{2,1,0:T(2,128)(2,1)}), bf16[64,2,8192]{2,1,0:T(2,128)(2,1)}, u32[]{:S(2)}, u32[]{:S(2)}) %all-to-all-start.2) | async-done | bytes 2097184 | tf_op jit(solution)/shard_map/all_to_all | solution.py:13
  126.9 8.0 %reshape.120 = bf16[64,8,32,64]{3,2,1,0:T(8,128)(2,1)} reshape(bf16[64,2,8192]{2,1,0:T(2,128)(2,1)} %all-to-all-done.2) | data formatting | bytes 4194304
  134.9 6.8 %copy.47 = bf16[8,32,64,64]{3,2,1,0:T(8,128)(2,1)} copy(bf16[8,32,64,64]{3,1,0,2:T(8,128)(2,1)} %bitcast.87) | data formatting | bytes 4194304 | tf_op jit(solution)/shard_map/reshape | solution.py:14
  141.7 6.6 %reshape_reshape.3 = bf16[256,4096]{1,0:T(8,128)(2,1)} reshape(bf16[8,32,64,64]{3,2,1,0:T(8,128)(2,1)} %copy.47) | data formatting | bytes 4194304 | tf_op jit(solution)/shard_map/reshape;reshape | solution.py:52
  148.3 9.3 %copy.45 = bf16[8,32,4096]{2,1,0:T(8,128)(2,1)} copy(bf16[8,32,4096]{1,0,2:T(8,128)(2,1)} %all-gather.3.cloned.1.call-done) | data formatting | bytes 4194304 | tf_op jit(solution)/shard_map/all_gather | solution.py:50
  157.7 2.5 fusion.2
  160.2 0.2 copy-done.3
  160.5 0.8 fusion.12
  161.3 54.7 %all-gather.5.cloned.1.call-done = bf16[4096,256]{1,0:T(8,128)(2,1)} async-done(((bf16[64,256]{1,0:T(8,128)(2,1)}), bf16[4096,256]{1,0:T(8,128)(2,1)}) %all-gather.5.cloned.1.call-update) | async-done | bytes 2097168 | tf_op jit(solution)/shard_map/all_gather | solution.py:81
  216.0 3.1 fusion.15
  219.1 1.3 fusion.34
  220.5 0.3 reduce-scatter.2.cloned.1.call-start
  220.7 2.9 fusion
  223.7 0.9 copy-done.2
  224.6 0.1 copy.49
  224.7 181.4 %all-reduce.3.cloned.1.call-done = f32[256,256]{0,1:T(8,128)} async-done(((f32[256,256]{0,1:T(8,128)}), f32[256,256]{0,1:T(8,128)}) %all-reduce.3.cloned.1.call-update) | async-done | bytes 262160 | tf_op jit(solution)/shard_map/psum | solution.py:90
  406.2 1.0 convert_add_fusion
  407.2 0.1 copy.51
  407.4 11.7 %cholesky.50 = f32[128,128]{1,0:T(8,128)S(1)} custom-call(f32[128,128]{1,0:T(8,128)S(1)} %cholesky.118), custom_call_target="Cholesky" | custom-call | tf_op jit(solution)/shard_map/jit(cholesky)/cholesky | solution.py:92
  419.1 9.8 %custom-call.18 = f32[1,128,128]{1,2,0:T(8,128)S(1)} custom-call(f32[1,128,128]{2,1,0:T(8,128)S(1)} %get-tuple-element.42), custom_call_target="InvertDiagBlocksLowerTriangular" | custom-call | tf_op jit(solution)/shard_map/jit(cholesky)/cholesky | solution.py:92
  429.0 0.2 constant_dynamic-update-slice_fusion.1
  429.2 0.3 convolution_subtract_fusion.2
  429.5 11.7 %cholesky.105 = f32[128,128]{1,0:T(8,128)S(1)} custom-call(f32[128,128]{1,0:T(8,128)S(1)} %convolution_subtract_fusion.2), custom_call_target="Cholesky" | custom-call | tf_op jit(solution)/shard_map/jit(cholesky)/cholesky | solution.py:92
  441.2 0.6 compare_reduce_fusion
  443.3 4.2 while.1
  443.5 0.6 fusion.57
  444.1 1.4 bitcast_dynamic-update-slice_fusion.2
  445.5 0.6 fusion.57
  446.1 1.4 bitcast_dynamic-update-slice_fusion.2
  447.5 19.7 %custom-call.19 = f32[2,128,128]{1,2,0:T(8,128)S(1)} custom-call(f32[2,128,128]{2,1,0:T(8,128)S(1)} %get-tuple-element.10), custom_call_target="InvertDiagBlocksLowerTriangular" | custom-call | tf_op jit(solution)/shard_map/jit(_cho_solve)/triangular_solve | solution.py:93
  467.2 0.2 fusion.19
  467.4 0.3 convolution_subtract_fusion.1
  467.7 0.2 fusion.27
  467.9 0.3 fusion.26
  468.2 0.3 convolution_subtract_fusion
  468.5 0.3 fusion.25
  468.7 93.1 %reduce-scatter.2.cloned.1.call-done = f32[256,64]{0,1:T(8,128)} async-done(((f32[256,4096]{0,1:T(8,128)}), f32[256,64]{0,1:T(8,128)}) %reduce-scatter.2.cloned.1.call-update) | async-done | bytes 65552 | tf_op jit(solution)/shard_map/reduce_scatter | solution.py:65
  561.9 0.8 convert_element_type.37
  562.7 0.1 copy.48
  562.8 0.7 reshape.121
  563.5 6.7 %all-to-all-start.3 = ((bf16[8,2,1024]{2,1,0:T(2,128)(2,1)}), bf16[8,2,1024]{2,1,0:T(2,128)(2,1)S(1)}, u32[]{:S(2)}, u32[]{:S(2)}) async-start(bf16[8,2,1024]{2,1,0:T(2,128)(2,1)} %reshape.121), calls=%async_computation.4 | async-start | bytes 65536 | tf_op jit(solution)/shard_map/all_to_all | solution.py:68
  570.3 0.7 maximum_bitcast_fusion
  571.0 0.8 copy.52
  571.8 6.5 %all-to-all-done.3 = bf16[8,2,1024]{2,1,0:T(2,128)(2,1)S(1)} async-done(((bf16[8,2,1024]{2,1,0:T(2,128)(2,1)}), bf16[8,2,1024]{2,1,0:T(2,128)(2,1)S(1)}, u32[]{:S(2)}, u32[]{:S(2)}) %all-to-all-start.3) | async-done | bytes 32800 | tf_op jit(solution)/shard_map/all_to_all | solution.py:68
  578.4 0.7 convolution_convert_fusion.2
  (33 shorter events, 1.0 us)
Async XLA Ops:
  7.2 150.5 %copy-start = (bf16[1,224,4096]{2,1,0:T(8,128)(2,1)S(1)}, bf16[1,224,4096]{2,1,0:T(8,128)(2,1)}, u32[]{:S(2)}) copy-start(bf16[1,224,4096]{2,1,0:T(8,128)(2,1)} %param.12) | copy-start | bytes 5505028
  7.2 141.2 %all-gather.3.cloned.1.call-start = ((), (), s32[]{:S(2)}) async-start(), calls=%async_computation.5 | async-start | bytes 8519680 | tf_op jit(solution)/shard_map/all_gather | solution.py:50
  49.7 77.2 %all-to-all-start.2 = ((bf16[64,2,8192]{2,1,0:T(2,128)(2,1)}), bf16[64,2,8192]{2,1,0:T(2,128)(2,1)}, u32[]{:S(2)}, u32[]{:S(2)}) async-start(bf16[64,2,8192]{2,1,0:T(2,128)(2,1)} %reshape.119), calls=%async_computation.2 | async-start | bytes 4194304 | tf_op jit(solution)/shard_map/all_to_all | solution.py:13
  63.7 152.2 %all-gather.5.cloned.1.call-start = ((), (), s32[]{:S(2)}) async-start(), calls=%async_computation.7 | async-start | bytes 2129920 | tf_op jit(solution)/shard_map/all_gather | solution.py:81
  64.5 341.7 %all-reduce.3.cloned.1.call-start = ((), (), s32[]{:S(2)}) async-start(), calls=%async_computation.8 | async-start | bytes 524288 | tf_op jit(solution)/shard_map/psum | solution.py:90
  157.7 2.5 copy-start.1
  157.7 2.8 copy-start.3
  220.5 341.4 %reduce-scatter.2.cloned.1.call-start = ((), (), s32[]{:S(2)}) async-start(), calls=%async_computation.6 | async-start | bytes 4259840 | tf_op jit(solution)/shard_map/reduce_scatter | solution.py:65
  223.6 0.9 copy-start.2
  563.5 14.8 %all-to-all-start.3 = ((bf16[8,2,1024]{2,1,0:T(2,128)(2,1)}), bf16[8,2,1024]{2,1,0:T(2,128)(2,1)S(1)}, u32[]{:S(2)}, u32[]{:S(2)}) async-start(bf16[8,2,1024]{2,1,0:T(2,128)(2,1)} %reshape.121), calls=%async_computation.4 | async-start | bytes 65536 | tf_op jit(solution)/shard_map/all_to_all | solution.py:68
Sparse Core Ops, SparseCore 0:
  27.3 108.4 all-gather.2
  139.1 76.7 all-gather.4
  220.6 185.5 all-reduce.2
  410.7 151.0 reduce-scatter.1
